TPU v7x, 256 devices: a whole 4x4x8 slice. The times are simulated.
256 devices in a mesh: gx: 16 (over z, core), gy: 16 (over y, x).
Axes of the slice: x: 4, y: 4, z: 8, core: 2. Of those that a mesh axis runs over, the one named last changes fastest.
Arguments:
- modes: float32 [524288, 512], P(('gx', 'gy'))
- batch: float32 [524288, 256], P(('gx', 'gy')), as said below
- core: float32 [768, 512], replicated, may hold values from -0.21875 to 0.21875
Outputs:
- new_modes: float32 [524288, 512], P(('gx', 'gy'))
Inputs may be any that keep to these rules, and one draw needn't show every extreme that they name: Each row of modes and batch shares one positive scale; batch holds a sizeable part of the span of modes.
All inputs are finite; a program needn't handle non-finite values.
Results may differ from a plain program's by a relative error of at most 0.000058.
Values sent between devices are 32-bit elements; how exact they have to be, the bound alone decides.
A program may use at most 64 MiB of HBM per device.

v0:
```python
import jax
import jax.numpy as jnp
from jax import lax
from jax.sharding import PartitionSpec as P


def matmul(left, right):
    return jnp.dot(left, right, precision=lax.Precision.HIGHEST, preferred_element_type=jnp.float32)


def global_sum(parts):
    return lax.psum((parts[0],), ("gx", "gy"))


def shards(modes, batch, core):
    total_rows = modes.shape[0] * lax.axis_size("gx") * lax.axis_size("gy")
    width = modes.shape[1]
    top = matmul(modes, core[:width])
    cross = global_sum((matmul(modes.T, batch),))[0]
    coeffs = cross / total_rows
    resid = batch - matmul(modes, coeffs)
    gram = global_sum((matmul(resid.T, resid),))[0] / total_rows
    lower = jnp.linalg.cholesky(gram)
    basis = jax.scipy.linalg.solve_triangular(lower, resid.T, lower=True).T
    return top + matmul(basis, core[width:])


def solution(mesh):
    placed = (P(("gx", "gy"), None), P(("gx", "gy"), None), P())
    return jax.shard_map(
        shards, mesh=mesh, in_specs=placed, out_specs=P(("gx", "gy"), None), check_vma=False
    )
```

profile of v0, /device:TPU:1, one launch (start us, length us, event | category | flops | bytes accessed | tf_op | source)
XLA Modules:
  0.0 619.0 jit_solution(16031329301337902461)
XLA Ops:
  6.5 0.0 copy-start.1
  6.5 0.0 all-reduce.4.cloned.1.call-start
  6.5 10.5 %fusion.20 = f32[512,256]{1,0:T(8,128)} fusion(f32[2048,512]{1,0:T(8,128)} %param.3, f32[2048,256]{1,0:T(8,128)} %param.4), kind=kOutput, calls=%fused_computation.42 | convolution fusion | flops 3221225472 | bytes 6815744 | tf_op jit(solution)/shard_map/dot_general | solution.py:8
  17.0 0.0 all-reduce.4.cloned.1.call-update
  17.0 0.5 all-reduce.6.cloned.1.call-start
  17.5 0.0 copy-done.1
  17.6 1.8 copy.4
  19.4 255.5 %all-reduce.4.cloned.1.call-done = f32[512,256]{1,0:T(8,128)} async-done(((f32[512,256]{1,0:T(8,128)}), f32[512,256]{1,0:T(8,128)}) %all-reduce.4.cloned.1.call-update) | async-done | bytes 524304 | tf_op jit(solution)/shard_map/psum | solution.py:12
  274.8 9.9 %fusion = f32[2048,256]{0,1:T(8,128)S(1)} fusion(f32[2048,256]{0,1:T(8,128)} %copy.4, f32[2048,512]{1,0:T(8,128)} %param.3, f32[512,256]{1,0:T(8,128)} %all-reduce.4.cloned.1.call-done), kind=kOutput, calls=%fused_computation.4 | convolution fusion | flops 3221880832 | bytes 8912896 | tf_op jit(solution)/shard_map/dot_general | solution.py:8
  284.8 2.6 fusion.21
  287.4 0.0 all-reduce.6.cloned.1.call-update
  287.4 10.2 %fusion.6 = f32[2048,512]{1,0:T(8,128)} fusion(f32[2048,512]{1,0:T(8,128)} %param.3, f32[768,512]{1,0:T(8,128)} %param.5), kind=kOutput, calls=%fused_computation.12 | convolution fusion | flops 6442450944 | bytes 9437184 | tf_op jit(solution)/shard_map/dot_general | solution.py:8
  297.6 242.8 %all-reduce.6.cloned.1.call-done = f32[256,256]{0,1:T(8,128)} async-done(((f32[256,256]{0,1:T(8,128)}), f32[256,256]{0,1:T(8,128)}) %all-reduce.6.cloned.1.call-update) | async-done | bytes 262160 | tf_op jit(solution)/shard_map/psum | solution.py:12
  540.5 1.0 broadcast_multiply_fusion
  541.4 0.1 copy.6
  541.6 1.0 fusion.10
  542.6 11.7 %cholesky.50 = f32[128,128]{1,0:T(8,128)S(1)} custom-call(f32[128,128]{1,0:T(8,128)S(1)} %cholesky.118), custom_call_target="Cholesky" | custom-call | tf_op jit(solution)/shard_map/jit(cholesky)/cholesky | solution.py:23
  554.3 9.8 %custom-call.15 = f32[1,128,128]{1,2,0:T(8,128)S(1)} custom-call(f32[1,128,128]{2,1,0:T(8,128)S(1)} %get-tuple-element.26), custom_call_target="InvertDiagBlocksLowerTriangular" | custom-call | tf_op jit(solution)/shard_map/jit(cholesky)/cholesky | solution.py:23
  564.2 0.2 constant_dynamic-update-slice_fusion.1
  564.4 0.3 convolution_subtract_fusion.1
  564.6 11.7 %cholesky.105 = f32[128,128]{1,0:T(8,128)S(1)} custom-call(f32[128,128]{1,0:T(8,128)S(1)} %convolution_subtract_fusion.1), custom_call_target="Cholesky" | custom-call | tf_op jit(solution)/shard_map/jit(cholesky)/cholesky | solution.py:23
  576.4 0.7 compare_reduce_fusion
  578.4 0.1 triangular_solve.57
  578.5 4.1 while.1
  578.5 0.7 fusion.33
  579.2 1.3 bitcast_dynamic-update-slice_fusion.2
  580.5 0.7 fusion.33
  581.2 1.3 bitcast_dynamic-update-slice_fusion.2
  582.5 19.9 %custom-call.16 = f32[2,128,128]{1,2,0:T(8,128)S(1)} custom-call(f32[2,128,128]{2,1,0:T(8,128)S(1)} %get-tuple-element.12), custom_call_target="InvertDiagBlocksLowerTriangular" | custom-call | tf_op jit(solution)/shard_map/jit(_solve_triangular)/triangular_solve | solution.py:24
  602.4 1.1 fusion.4
  603.5 0.0 copy-start
  603.5 1.0 convolution_subtract_fusion
  604.5 1.0 fusion.13
  605.6 0.1 copy-done
  605.7 6.2 %convolution_add_fusion = f32[2048,512]{1,0:T(8,128)} fusion(f32[2048,512]{1,0:T(8,128)S(1)} %copy-done, f32[128,2048]{1,0:T(8,128)S(1)} %fusion.13, f32[128,2048]{1,0:T(8,128)S(1)} %fusion.4, f32[768,512]{1,0:T(8,128)} %param.5), kind=kOutput, calls=%fused_computation.2 | convolution fusion | flops 3222798336 | bytes 11010048 | tf_op jit(solution)/shard_map/dot_general | solution.py:8
  (9 shorter events, 0.1 us)
Async XLA Ops:
  6.5 11.0 %copy-start.1 = (f32[2048,256]{1,0:T(8,128)S(1)}, f32[2048,256]{1,0:T(8,128)}, u32[]{:S(2)}) copy-start(f32[2048,256]{1,0:T(8,128)} %param.4) | copy-start | bytes 6291460
  6.5 268.3 %all-reduce.4.cloned.1.call-start = ((), (), s32[]{:S(2)}) async-start(), calls=%async_computation | async-start | bytes 1048576 | tf_op jit(solution)/shard_map/psum | solution.py:12
  17.0 523.4 %all-reduce.6.cloned.1.call-start = ((), (), s32[]{:S(2)}) async-start(), calls=%async_computation.1 | async-start | bytes 524288 | tf_op jit(solution)/shard_map/psum | solution.py:12
  603.5 2.2 copy-start
Sparse Core Ops, SparseCore 0:
  17.2 257.6 all-reduce.3
  287.5 252.9 all-reduce.5
where the time goes:
time: 625 us; the launch traced here: 619 us
  waiting for transfers between devices  498 us (80%)
  other arithmetic  55.9 us (9%)
  matrix products  43 us (7%)
  between operations  15 us (2%)
    psum x2, waiting for transfers between devices, global_sum(): return lax.psum((parts[0],), ('gx', 'gy'))  498 us
    dot_general x5, matrix products, matmul(): jnp.dot(left, right, precision=lax.Precision.HIGHEST, preferred_element_t...  39.4 us
    another operation x6, other arithmetic, shards(): lower = jnp.linalg.cholesky(gram)  34 us
    another operation x3, other arithmetic, shards(): basis = jax.scipy.linalg.solve_triangular(lower, resid.T, lower=True).T  19.9 us
  transfers between devices with their start and end apart: 2, of which 2 were waited for; matrix products, arithmetic and copies ran while one was open for 2% of the time, Pallas kernels for 0%

commit v1 on v0

v1 whole, which is shorter than its diff:
```python
import functools

import jax
import jax.numpy as jnp
from jax import lax
from jax.experimental import pallas as pl
from jax.experimental.pallas import tpu as pltpu
from jax.sharding import PartitionSpec as P

MESH = pl.DeviceIdType.MESH
NZ, NY, NX = 8, 4, 4
PAIRS = ((0, 0), (0, 1), (1, 1), (0, 2), (1, 2), (2, 2))
PANELS = 2 * len(PAIRS)


def split(value):
    high = value.astype(jnp.bfloat16)
    low = (value - high.astype(jnp.float32)).astype(jnp.bfloat16)
    return high, low


def gram_kernel(modes_ref, batch_ref, gram_ref):
    @pl.when(pl.program_id(0) == 0)
    def _():
        gram_ref[...] = jnp.zeros_like(gram_ref)

    groups = (modes_ref[:, :256], modes_ref[:, 256:], batch_ref[...])
    parts = [split(group) for group in groups]
    flipped = [(high.T, low.T) for high, low in parts]
    for index, (i, j) in enumerate(PAIRS):
        high_t, low_t = flipped[i]
        high, low = parts[j]
        block = jnp.dot(high_t, low, preferred_element_type=jnp.float32)
        block += jnp.dot(low_t, high, preferred_element_type=jnp.float32)
        block += jnp.dot(high_t, high, preferred_element_type=jnp.float32)
        gram_ref[2 * index] += block[:, :128]
        gram_ref[2 * index + 1] += block[:, 128:]


def local_gram(modes, batch, tile=512):
    rows, width = modes.shape
    return pl.pallas_call(
        gram_kernel,
        grid=(rows // tile,),
        in_specs=[
            pl.BlockSpec((tile, width), lambda i: (i, 0)),
            pl.BlockSpec((tile, batch.shape[1]), lambda i: (i, 0)),
        ],
        out_specs=pl.BlockSpec((PANELS, 256, 128), lambda i: (0, 0, 0)),
        out_shape=jax.ShapeDtypeStruct((PANELS, 256, 128), jnp.float32),
        compiler_params=pltpu.CompilerParams(dimension_semantics=("arbitrary",)),
        name="gram",
    )(modes, batch)


def sum_kernel(
    part, out, from_core, half, from_first, quarter, from_second, mine, from_z,
    core_send, core_recv, first_send, first_recv, second_send, second_recv, z_send, z_recv,
    gather_second, gather_first, gather_core, arrived,
):
    gx, gy = lax.axis_index("gx"), lax.axis_index("gy")
    z, core = gx // 2, gx % 2
    y, x = gy // NX, gy % NX
    partner = (z * 2 + (1 - core), gy)
    first, second = (x, y), (y, x)

    def along(axis, index):
        return (gx, y * NX + index) if axis == 0 else (gx, index * NX + x)

    def at_z(index):
        return (index * 2 + core, gy)

    def copy(src, dst, send, recv, device):
        return pltpu.make_async_remote_copy(
            src_ref=src, dst_ref=dst, send_sem=send, recv_sem=recv,
            device_id=device, device_id_type=MESH,
        )

    barrier = pltpu.get_barrier_semaphore()
    peers = [partner]
    peers += [along(0, (x + d) % NX) for d in range(1, NX)]
    peers += [along(1, (y + d) % NY) for d in range(1, NY)]
    peers += [at_z((z + d) % NZ) for d in range(1, NZ)]
    for peer in peers:
        pl.semaphore_signal(barrier, inc=1, device_id=peer, device_id_type=MESH)
    pl.semaphore_wait(barrier, len(peers))

    sent = []

    def start(c):
        c.start()
        sent.append(c)
        return c

    core_copies = {}
    for d in (2, 1, 3, 0):
        for p in (0, 1):
            a = (first[p] + d) % 4
            core_copies[p, d] = start(copy(
                part.at[1 - core, p, a], from_core.at[p, a], core_send.at[p, d], core_recv.at[p, d], partner))

    first_copies = {}
    for d in (2, 1, 3, 0):
        for p in (0, 1):
            a = (first[p] + d) % 4
            core_copies[p, d].wait_recv()
            half[p, d] = part[core, p, a] + from_core[p, a]
            if d:
                first_copies[p, d] = start(copy(
                    half.at[p, d], from_first.at[p, d - 1], first_send.at[p, d - 1], first_recv.at[p, d - 1],
                    along(p, a)))

    second_copies = {}
    for p in (0, 1):
        for d in (2, 1, 3):
            first_copies[p, d].wait_recv()
        for d in (2, 1, 3, 0):
            b = (second[p] + d) % 4
            quarter[p, d] = (
                half[p, 0, b] + from_first[p, 0, b]) + (from_first[p, 1, b] + from_first[p, 2, b])
            if d:
                second_copies[p, d] = start(copy(
                    quarter.at[p, d], from_second.at[p, d - 1], second_send.at[p, d - 1],
                    second_recv.at[p, d - 1], along(1 - p, b)))

    for p in (0, 1):
        for d in (2, 1, 3):
            second_copies[p, d].wait_recv()
        mine[p] = (quarter[p, 0] + from_second[p, 0]) + (from_second[p, 1] + from_second[p, 2])

    z_copies = {}
    for d in (4, 3, 5, 2, 6, 1, 7):
        z_copies[d] = start(copy(
            mine, from_z.at[z], z_send.at[d - 1], z_recv.at[d - 1], at_z((z + d) % NZ)))
    from_z[z] = mine[...]
    for d in (1, 7, 2, 6, 3, 5, 4):
        z_copies[d].wait_recv()

    def place(owner, p, a, b):
        return (owner, p, a, b)

    for p in (0, 1):
        here = (core, p, first[p], second[p])
        total = from_z[0, p]
        for index in range(1, NZ):
            total = total + from_z[index, p]
        out[here] = total
        for d in (2, 1, 3):
            start(copy(out.at[here], out.at[here], gather_second.at[p, d - 1], arrived.at[here],
                       along(1 - p, (second[p] + d) % 4)))
        for d in (2, 1, 3):
            start(copy(out.at[here], out.at[here], gather_first.at[p, 0, d - 1], arrived.at[here],
                       along(p, (first[p] + d) % 4)))
        start(copy(out.at[here], out.at[here], gather_core.at[p, 0, 0], arrived.at[here], partner))

    def received(piece):
        copy(out.at[piece], out.at[piece], gather_core.at[0, 0, 0], arrived.at[piece], partner).wait_recv()

    for e in (1, 3, 2):
        for p in (0, 1):
            piece = (core, p, first[p], (second[p] + e) % 4)
            received(piece)
            for d in (2, 1, 3):
                start(copy(out.at[piece], out.at[piece], gather_first.at[p, e, d - 1], arrived.at[piece],
                           along(p, (first[p] + d) % 4)))
            start(copy(out.at[piece], out.at[piece], gather_core.at[p, 0, e], arrived.at[piece], partner))

    for e in (0, 1, 3, 2):
        for d in (1, 3, 2):
            for p in (0, 1):
                piece = (core, p, (first[p] + d) % 4, (second[p] + e) % 4)
                received(piece)
                start(copy(out.at[piece], out.at[piece], gather_core.at[p, d, e], arrived.at[piece], partner))

    for d in range(4):
        for e in range(4):
            for p in (0, 1):
                received((1 - core, p, (first[p] + d) % 4, (second[p] + e) % 4))
    for c in sent:
        c.wait_send()


def global_sum(part):
    rows = part.shape[0] * part.shape[1] // 64
    f32 = jnp.float32
    vmem = pl.BlockSpec(memory_space=pltpu.VMEM)
    dma = pltpu.SemaphoreType.DMA
    out = pl.pallas_call(
        sum_kernel,
        in_specs=[vmem],
        out_specs=vmem,
        out_shape=jax.ShapeDtypeStruct((2, 2, 4, 4, rows, 128), f32),
        scratch_shapes=[
            pltpu.VMEM((2, 4, 4, rows, 128), f32),
            pltpu.VMEM((2, 4, 4, rows, 128), f32),
            pltpu.VMEM((2, 3, 4, rows, 128), f32),
            pltpu.VMEM((2, 4, rows, 128), f32),
            pltpu.VMEM((2, 3, rows, 128), f32),
            pltpu.VMEM((2, rows, 128), f32),
            pltpu.VMEM((NZ, 2, rows, 128), f32),
            dma((2, 4)), dma((2, 4)), dma((2, 3)), dma((2, 3)), dma((2, 3)), dma((2, 3)),
            dma((NZ - 1,)), dma((NZ - 1,)),
            dma((2, 3)), dma((2, 4, 3)), dma((2, 4, 4)), dma((2, 2, 4, 4)),
        ],
        compiler_params=pltpu.CompilerParams(collective_id=0, has_side_effects=True),
        name="global_sum",
    )(part.reshape(2, 2, 4, 4, rows, 128))
    return out.reshape(part.shape)


def matmul(left, right, precision=lax.Precision.HIGHEST):
    return jnp.dot(left, right, precision=precision, preferred_element_type=jnp.float32)


def shards(modes, batch, core):
    total_rows = modes.shape[0] * lax.axis_size("gx") * lax.axis_size("gy")
    width = modes.shape[1]
    sums = global_sum(local_gram(modes, batch))
    block = {pair: jnp.concatenate([sums[2 * i], sums[2 * i + 1]], axis=1) for i, pair in enumerate(PAIRS)}
    modes_modes = jnp.block([[block[0, 0], block[0, 1]], [block[0, 1].T, block[1, 1]]])
    modes_batch = jnp.concatenate([block[0, 2], block[1, 2]], axis=0)
    coeffs = modes_batch / total_rows
    gram = (block[2, 2] - matmul(coeffs.T, 2.0 * modes_batch - matmul(modes_modes, coeffs))) / total_rows
    lower = jnp.linalg.cholesky(gram)
    inverse = jax.scipy.linalg.solve_triangular(lower, jnp.eye(lower.shape[0], dtype=jnp.float32), lower=True)
    weights = matmul(inverse.T, core[width:])
    top = core[:width] - matmul(coeffs, weights)
    high = lax.Precision.HIGH
    return matmul(modes, top, high) + matmul(batch, weights, high)


def solution(mesh):
    placed = (P(("gx", "gy"), None), P(("gx", "gy"), None), P())
    return jax.shard_map(
        shards, mesh=mesh, in_specs=placed, out_specs=P(("gx", "gy"), None), check_vma=False
    )
```

time: 625 us -> 141 us (0.23)
  waiting for transfers between devices: 498 us -> 0 us
  Pallas kernels: 0 us -> 54.7 us
  matrix products: 43 us -> 18.5 us
  between operations: 15 us -> 1.63 us
    psum x2 -> x0, waiting for transfers between devices: 498 us -> none  [global_sum(): return lax.psum((parts[0],), ('gx', 'gy'))]
    pallas_call x0 -> x2, Pallas kernels: none -> 54.7 us  [the longest x1 46.3 us: global_sum(): pl.pallas_call(sum_kernel, in_specs=[vmem], out_specs=vmem, out_shape=jax...]
    dot_general x5 -> x6, matrix products: 39.4 us -> 17.2 us  [matmul(): jnp.dot(left, right, precision=precision, preferred_element_type=jnp.floa...]
  transfers between devices with their start and end apart: 2 -> 0, of which waited for: 2 -> 0; matrix products, arithmetic and copies ran while one was open for 2% -> 0% of each run, Pallas kernels for 0% -> 0%
where the time goes in v1:
time: 141 us
  Pallas kernels  54.7 us (39%)
  other arithmetic  54 us (38%)
  matrix products  18.5 us (13%)
  local copies, waits for them, and re-layouts  12 us (9%)
  between operations  1.63 us (1%)
    pallas_call x1, Pallas kernels, global_sum(): pl.pallas_call(sum_kernel, in_specs=[vmem], out_specs=vmem, out_shape=jax...  46.3 us
    another operation x6, other arithmetic, shards(): lower = jnp.linalg.cholesky(gram)  34.2 us
    another operation x3, other arithmetic, shards(): jax.scipy.linalg.solve_triangular(lower, jnp.eye(lower.shape[0], dtype=jn...  19.7 us
    dot_general x6, matrix products, matmul(): jnp.dot(left, right, precision=precision, preferred_element_type=jnp.floa...  17.2 us
    pallas_call x1, Pallas kernels, local_gram(): pl.pallas_call(gram_kernel, grid=(rows // tile,), in_specs=[pl.BlockSpec(...  8.4 us
    add x1, local copies, waits for them, and re-layouts, shards(): return matmul(modes, top, high) + matmul(batch, weights, high)  5.34 us
    another operation x6, local copies, waits for them, and re-layouts  4.06 us

profile of v1, /device:TPU:1, one launch (start us, length us, event | category | flops | bytes accessed | tf_op | source)
XLA Modules:
  0.0 140.8 jit_solution(14905679819527918960)
XLA Ops:
  0.0 0.1 triangular_solve.63
  0.1 8.4 %gram.1 = f32[12,256,128]{2,1,0:T(8,128)} custom-call(f32[2048,512]{1,0:T(8,128)} %modes_ref.1, f32[2048,256]{1,0:T(8,128)} %batch_ref.1), custom_call_target="tpu_custom_call" | custom-call | tf_op jit(solution)/shard_map/gram/pallas_call | solution.py:42
  8.5 46.3 %global_sum.1 = f32[2,2,4,4,48,128]{5,4,3,2,1,0:T(8,128)} custom-call(f32[2,2,4,4,48,128]{5,4,3,2,1,0:T(8,128)} %bitcast.65), custom_call_target="tpu_custom_call" | custom-call | tf_op jit(solution)/shard_map/global_sum/pallas_call | solution.py:188
  54.8 1.6 %fusion.41 = (f32[1,256,128]{2,1,0:T(8,128)S(1)}, f32[256,128]{1,0:T(8,128)S(1)}, f32[1,256,128]{2,1,0:T(8,128)S(1)}, f32[1,256,128]{2,1,0:T(8,128)S(1)}, f32[1,...) fusion(f32[12,256,128]{2,1,0:T(8,128)} %bitcast.64), kind=kLoop, calls=%fused_computation.75 | loop fusion | bytes 3276800 | tf_op jit(solution)/shard_map/slice | solution.py:219
  56.4 0.1 copy.27
  56.5 0.1 copy.30
  56.6 0.1 copy.29
  56.7 0.1 copy.28
  56.8 0.1 copy.21
  56.9 0.1 copy.22
  57.0 0.1 copy.31
  57.1 0.1 copy.19
  57.3 1.8 %convolution_subtract_fusion.1 = f32[512,256]{1,0:T(8,128)S(1)} fusion(f32[256,128]{0,1:T(8,128)S(1)} %copy.22, f32[256,128]{0,1:T(8,128)S(1)} %copy.21, f32[256,256]{0,1:T(8,128)S(1)} %maximum_bitcast_fusion, f32[256,128]{0,1:T(8,128)S(1)} %copy.19, f32[256,128]{0,1:T(8,128)S(1)} %bitcast.70, f32[256,128]{0,1:T(8,128)S(1)} %bitcast.68, ...), kind=kOutput, calls=%fused_computation.4 | convolution fusion | flops 808058880 | bytes 2097152 | tf_op jit(solution)/shard_map/dot_general | solution.py:212
  59.1 0.0 copy-start.2
  59.1 1.0 fusion
  60.1 0.1 copy.24
  60.3 11.7 %cholesky.50 = f32[128,128]{1,0:T(8,128)S(1)} custom-call(f32[128,128]{1,0:T(8,128)S(1)} %cholesky.118), custom_call_target="Cholesky" | custom-call | tf_op jit(solution)/shard_map/jit(cholesky)/cholesky | solution.py:224
  72.1 9.8 %custom-call.15 = f32[1,128,128]{1,2,0:T(8,128)S(1)} custom-call(f32[1,128,128]{2,1,0:T(8,128)S(1)} %get-tuple-element.39), custom_call_target="InvertDiagBlocksLowerTriangular" | custom-call | tf_op jit(solution)/shard_map/jit(cholesky)/cholesky | solution.py:224
  81.9 0.2 constant_dynamic-update-slice_fusion.1
  82.1 0.3 convolution_subtract_fusion.4
  82.4 11.9 %cholesky.105 = f32[128,128]{1,0:T(8,128)S(1)} custom-call(f32[128,128]{1,0:T(8,128)S(1)} %convolution_subtract_fusion.4), custom_call_target="Cholesky" | custom-call | tf_op jit(solution)/shard_map/jit(cholesky)/cholesky | solution.py:224
  94.3 0.7 compare_reduce_fusion
  96.4 4.1 %while.1 = (s32[]{:T(128)}, f32[256,256]{1,0:T(8,128)S(1)}, s32[2,2]{1,0:T(2,128)S(1)}, f32[2,128,128]{2,1,0:T(8,128)S(1)}, s32[]{:T(128)}) while((s32[]{:T(128)}, f32[256,256]{1,0:T(8,128)S(1)}, s32[2,2]{1,0:T(2,128)S(1)}, f32[2,128,128]{2,1,0:T(8,128)S(1)}, s32[]{:T(128)}) %tuple.35), condition=%wide.while_cond, body=%wide.while_body.sunk | while | flops 2 | bytes 131189 | solution.py:225
  96.5 0.6 fusion.54
  97.1 1.4 %bitcast_dynamic-update-slice_fusion.2 = f32[2,128,128]{2,1,0:T(8,128)S(1)} fusion(f32[2,128,128]{2,1,0:T(8,128)S(1)} %get-tuple-element.81, s32[]{:T(128)S(6)} %copy.38, f32[256,256]{1,0:T(8,128)S(1)} %get-tuple-element.84, s32[]{:T(128)} %bitcast.62, s32[]{:T(128)} %bitcast.63), kind=kLoop, calls=%fused_computation.clone.1 | loop fusion | bytes 131084 | tf_op jit(solution)/shard_map/jit(_solve_triangular)/triangular_solve
  98.5 0.6 fusion.54
  99.1 1.4 %bitcast_dynamic-update-slice_fusion.2 = f32[2,128,128]{2,1,0:T(8,128)S(1)} fusion(f32[2,128,128]{2,1,0:T(8,128)S(1)} %get-tuple-element.81, s32[]{:T(128)S(6)} %copy.38, f32[256,256]{1,0:T(8,128)S(1)} %get-tuple-element.84, s32[]{:T(128)} %bitcast.62, s32[]{:T(128)} %bitcast.63), kind=kLoop, calls=%fused_computation.clone.1 | loop fusion | bytes 131084 | tf_op jit(solution)/shard_map/jit(_solve_triangular)/triangular_solve
  100.6 19.7 %custom-call.16 = f32[2,128,128]{1,2,0:T(8,128)S(1)} custom-call(f32[2,128,128]{2,1,0:T(8,128)S(1)} %get-tuple-element.12), custom_call_target="InvertDiagBlocksLowerTriangular" | custom-call | tf_op jit(solution)/shard_map/jit(_solve_triangular)/triangular_solve | solution.py:225
  120.2 0.0 copy-start
  120.2 0.3 fusion.26
  120.5 0.3 convolution_subtract_fusion.3
  120.8 0.3 fusion.29
  121.1 0.0 copy-done.2
  121.1 0.6 fusion.14
  121.8 1.1 convolution_subtract_fusion
  122.8 0.0 copy-done
  122.9 0.0 copy-start.1
  122.9 6.9 %fusion.42 = f32[512,2048]{1,0:T(8,128)S(1)} fusion(f32[512,512]{1,0:T(8,128)S(1)} %convolution_subtract_fusion, f32[2048,512]{1,0:T(8,128)S(1)} %copy-done), kind=kOutput, calls=%fused_computation.76 | convolution fusion | flops 3221225472 | bytes 9437184 | tf_op jit(solution)/shard_map/dot_general | solution.py:212
  129.8 0.0 copy-done.1
  129.8 5.7 %add_bitcast_fusion = f32[2048,512]{0,1:T(8,128)} fusion(f32[512,2048]{1,0:T(8,128)S(1)} %fusion.42, f32[256,512]{1,0:T(8,128)S(1)} %fusion.14, f32[2048,256]{1,0:T(8,128)S(1)} %copy-done.1), kind=kOutput, calls=%fused_computation.2 | convolution fusion | flops 1611661312 | bytes 11010048 | tf_op jit(solution)/shard_map/dot_general | solution.py:212
  135.5 5.3 %copy.25 = f32[2048,512]{1,0:T(8,128)} copy(f32[2048,512]{0,1:T(8,128)} %add_bitcast_fusion) | data formatting | bytes 8388608 | tf_op jit(solution)/shard_map/add | solution.py:229
  (12 shorter events, 0.2 us)
Async XLA Ops:
  59.1 62.0 %copy-start.2 = (f32[768,512]{1,0:T(8,128)S(1)}, f32[768,512]{1,0:T(8,128)}, u32[]{:S(2)}) copy-start(f32[768,512]{1,0:T(8,128)} %param.5) | copy-start | bytes 4718596
  120.2 2.6 %copy-start = (f32[2048,512]{1,0:T(8,128)S(1)}, f32[2048,512]{1,0:T(8,128)}, u32[]{:S(2)}) copy-start(f32[2048,512]{1,0:T(8,128)} %modes_ref.1) | copy-start | bytes 12582916
  122.9 7.0 %copy-start.1 = (f32[2048,256]{1,0:T(8,128)S(1)}, f32[2048,256]{1,0:T(8,128)}, u32[]{:S(2)}) copy-start(f32[2048,256]{1,0:T(8,128)} %batch_ref.1) | copy-start | bytes 6291460

commit v2 on v1

--- a/solution.py
+++ b/solution.py
@@ -11,6 +11,7 @@
 NZ, NY, NX = 8, 4, 4
 PAIRS = ((0, 0), (0, 1), (1, 1), (0, 2), (1, 2), (2, 2))
 PANELS = 2 * len(PAIRS)
+BLOCK = 64
 
 
 def split(value):
@@ -208,25 +209,138 @@
     return out.reshape(part.shape)
 
 
-def matmul(left, right, precision=lax.Precision.HIGHEST):
-    return jnp.dot(left, right, precision=precision, preferred_element_type=jnp.float32)
+def exact_dot(a, b, dims=((1,), (0,))):
+    return lax.dot_general(a, b, (dims, ((), ())), precision=lax.Precision.HIGHEST, preferred_element_type=jnp.float32)
+
+def lanes(value, index):
+    return jnp.broadcast_to(value[:, index:index + 1], value.shape)
+
+def row_of(value, index):
+    return jnp.broadcast_to(value[index:index + 1, :], value.shape)
+
+def eliminate(tiles, offset):
+    shape = tiles[0].shape
+    sub = lax.broadcasted_iota(jnp.int32, shape, 0)
+    scales = []
+    for g in range(len(tiles)):
+        w = tiles[g]
+        c = [lanes(w, offset + 8 * g + j) for j in range(8)]
+        rows, inv, s = [], [], {}
+        pivots = jnp.ones(shape, jnp.float32)
+        for j in range(8):
+            row = row_of(w, j)
+            pivot = row_of(c[j], j)
+            r = 1.0 / pivot
+            pivots = jnp.where(sub == j, pivot, pivots)
+            m = jnp.where(sub > j, c[j] * r, 0.0)
+            w = w - m * row
+            for k in range(j + 1, 8):
+                s[j, k] = row_of(c[k], j)
+                c[k] = c[k] - m * s[j, k]
+            rows.append(row)
+            inv.append(r)
+        tiles[g] = w
+        scales.append(lax.rsqrt(pivots))
+        for h in range(g + 1, len(tiles)):
+            v = tiles[h]
+            c = [lanes(v, offset + 8 * g + j) for j in range(8)]
+            for j in range(8):
+                m = c[j] * inv[j]
+                v = v - m * rows[j]
+                for k in range(j + 1, 8):
+                    c[k] = c[k] - m * s[j, k]
+            tiles[h] = v
+    return [t * q for t, q in zip(tiles, scales)]
+
+
+def factor(aug):
+    n = aug.shape[0]
+    for d in range(n // BLOCK):
+        o = BLOCK * d
+        tile = o // 128 * 128
+        odd = d % 2
+        block = aug[o:o + BLOCK, tile:tile + 128]
+        lane = lax.broadcasted_iota(jnp.int32, (BLOCK, 128), 1)
+        row = lax.broadcasted_iota(jnp.int32, (BLOCK, 128), 0)
+        eye = jnp.where(lane == row + (0 if odd else 64), 1.0, 0.0)
+        w = jnp.where((lane >= 64) if odd else (lane < 64), block, eye)
+        tiles = eliminate([w[8 * g:8 * g + 8] for g in range(BLOCK // 8)], 64 if odd else 0)
+        w = jnp.concatenate(tiles, axis=0)
+        if not odd:
+            w = pltpu.roll(w, 64, 1)
+        z = w[:, :64]
+        new = exact_dot(z, aug[o:o + BLOCK, :])
+        aug[o:o + BLOCK, :] = new
+        if o + BLOCK < n:
+            rest = new[:, :n]
+            upd = exact_dot(rest, new, ((0,), (0,)))
+            aug[o + BLOCK:, :] = aug[o + BLOCK:, :] - upd[o + BLOCK:, :]
+
+def update_kernel(total_rows, sums_ref, core_ref, modes_ref, batch_ref, out_ref, aug, high, low):
+    width = modes_ref.shape[1]
+    n = batch_ref.shape[1]
+
+    @pl.when(pl.program_id(0) == 0)
+    def _():
+        def block(index):
+            return jnp.concatenate([sums_ref[2 * index], sums_ref[2 * index + 1]], axis=1)
+
+        first, second = block(3), block(4)
+        coeffs = (first * (1.0 / total_rows), second * (1.0 / total_rows))
+        mixed = block(1)
+        product_first = exact_dot(block(0), coeffs[0]) + exact_dot(mixed, coeffs[1])
+        product_second = exact_dot(mixed, coeffs[0], ((0,), (0,))) + exact_dot(block(2), coeffs[1])
+        gram = block(5) - exact_dot(coeffs[0], 2.0 * first - product_first, ((0,), (0,)))
+        gram = gram - exact_dot(coeffs[1], 2.0 * second - product_second, ((0,), (0,)))
+        aug[:, :n] = gram * (1.0 / total_rows)
+        row = lax.broadcasted_iota(jnp.int32, (n, n), 0)
+        column = lax.broadcasted_iota(jnp.int32, (n, n), 1)
+        aug[:, n:] = jnp.where(row == column, 1.0, 0.0)
+        factor(aug)
+        weights = exact_dot(aug[:, n:], core_ref[width:, :], ((0,), (0,)))
+        high[width:, :], low[width:, :] = split(weights)
+        for i in range(width // n):
+            top = core_ref[n * i:n * (i + 1), :] - exact_dot(coeffs[i], weights)
+            high[n * i:n * (i + 1), :], low[n * i:n * (i + 1), :] = split(top)
+
+    modes_high, modes_low = split(modes_ref[...])
+    batch_high, batch_low = split(batch_ref[...])
+
+    def times(left, right):
+        return jnp.dot(left, right, preferred_element_type=jnp.float32)
+
+    small = times(modes_low, high[:width, :]) + times(batch_low, high[width:, :])
+    small += times(modes_high, low[:width, :]) + times(batch_high, low[width:, :])
+    out_ref[...] = small + times(modes_high, high[:width, :]) + times(batch_high, high[width:, :])
+
+
+def update(sums, core, modes, batch, total_rows, tile=256):
+    rows, width = modes.shape
+    n = batch.shape[1]
+    return pl.pallas_call(
+        functools.partial(update_kernel, total_rows),
+        grid=(rows // tile,),
+        in_specs=[
+            pl.BlockSpec(sums.shape, lambda i: (0, 0, 0), pipeline_mode=pl.Buffered(1)),
+            pl.BlockSpec(core.shape, lambda i: (0, 0), pipeline_mode=pl.Buffered(1)),
+            pl.BlockSpec((tile, width), lambda i: (i, 0)),
+            pl.BlockSpec((tile, n), lambda i: (i, 0)),
+        ],
+        out_specs=pl.BlockSpec((tile, width), lambda i: (i, 0)),
+        out_shape=jax.ShapeDtypeStruct((rows, width), jnp.float32),
+        scratch_shapes=[
+            pltpu.VMEM((n, 2 * n), jnp.float32),
+            pltpu.VMEM(core.shape, jnp.bfloat16),
+            pltpu.VMEM(core.shape, jnp.bfloat16),
+        ],
+        compiler_params=pltpu.CompilerParams(dimension_semantics=("arbitrary",)),
+        name="update",
+    )(sums, core, modes, batch)
 
 
 def shards(modes, batch, core):
     total_rows = modes.shape[0] * lax.axis_size("gx") * lax.axis_size("gy")
-    width = modes.shape[1]
-    sums = global_sum(local_gram(modes, batch))
-    block = {pair: jnp.concatenate([sums[2 * i], sums[2 * i + 1]], axis=1) for i, pair in enumerate(PAIRS)}
-    modes_modes = jnp.block([[block[0, 0], block[0, 1]], [block[0, 1].T, block[1, 1]]])
-    modes_batch = jnp.concatenate([block[0, 2], block[1, 2]], axis=0)
-    coeffs = modes_batch / total_rows
-    gram = (block[2, 2] - matmul(coeffs.T, 2.0 * modes_batch - matmul(modes_modes, coeffs))) / total_rows
-    lower = jnp.linalg.cholesky(gram)
-    inverse = jax.scipy.linalg.solve_triangular(lower, jnp.eye(lower.shape[0], dtype=jnp.float32), lower=True)
-    weights = matmul(inverse.T, core[width:])
-    top = core[:width] - matmul(coeffs, weights)
-    high = lax.Precision.HIGH
-    return matmul(modes, top, high) + matmul(batch, weights, high)
+    return update(global_sum(local_gram(modes, batch)), core, modes, batch, total_rows)
 
 
 def solution(mesh):

time: 141 us -> 79.3 us (0.56)
  other arithmetic: 54 us -> 0 us
  Pallas kernels: 54.7 us -> 79 us
  matrix products: 18.5 us -> 0 us
  local copies, waits for them, and re-layouts: 12 us -> 0 us
  between operations: 1.63 us -> 0.01 us
    another operation x9 -> x0, other arithmetic: 53.9 us -> none  [the longest x6 34.2 us: shards(): lower = jnp.linalg.cholesky(gram)]
    pallas_call x0 -> x1, Pallas kernels: none -> 24.3 us  [update(): pl.pallas_call(functools.partial(update_kernel, total_rows), grid=(rows /...]
    dot_general x6 -> x0, matrix products: 17.2 us -> none  [matmul(): jnp.dot(left, right, precision=precision, preferred_element_type=jnp.floa...]
    add x1 -> x0, local copies, waits for them, and re-layouts: 5.34 us -> none  [shards(): return matmul(modes, top, high) + matmul(batch, weights, high)]
    another operation x9 -> x0, local copies, waits for them, and re-layouts: 4.16 us -> none
    slice x1 -> x0, local copies, waits for them, and re-layouts: 1.6 us -> none  [shards(): sums[2 * i]]
where the time goes in v2:
time: 79.3 us; the launch traced here: 79 us
  Pallas kernels  79 us (100%)
    pallas_call x1, Pallas kernels, global_sum(): pl.pallas_call(sum_kernel, in_specs=[vmem], out_specs=vmem, out_shape=jax...  46.3 us
    pallas_call x1, Pallas kernels, update(): pl.pallas_call(functools.partial(update_kernel, total_rows), grid=(rows /...  24.3 us
    pallas_call x1, Pallas kernels, local_gram(): pl.pallas_call(gram_kernel, grid=(rows // tile,), in_specs=[pl.BlockSpec(...  8.39 us

profile of v2, /device:TPU:1, one launch (start us, length us, event | category | flops | bytes accessed | tf_op | source)
XLA Modules:
  0.0 79.0 jit_solution(13054551904557503428)
XLA Ops:
  0.0 8.4 %gram.1 = f32[12,256,128]{2,1,0:T(8,128)} custom-call(f32[2048,512]{1,0:T(8,128)} %modes_ref.3, f32[2048,256]{1,0:T(8,128)} %batch_ref.3), custom_call_target="tpu_custom_call" | custom-call | tf_op jit(solution)/shard_map/gram/pallas_call | solution.py:43
  8.4 46.3 %global_sum.1 = f32[2,2,4,4,48,128]{5,4,3,2,1,0:T(8,128)} custom-call(f32[2,2,4,4,48,128]{5,4,3,2,1,0:T(8,128)} %bitcast.3), custom_call_target="tpu_custom_call" | custom-call | tf_op jit(solution)/shard_map/global_sum/pallas_call | solution.py:189
  54.7 24.3 %update.1 = f32[2048,512]{1,0:T(8,128)} custom-call(f32[12,256,128]{2,1,0:T(8,128)} %bitcast.2, f32[768,512]{1,0:T(8,128)} %core_ref.1, f32[2048,512]{1,0:T(8,128)} %modes_ref.3, f32[2048,256]{1,0:T(8,128)} %batch_ref.3), custom_call_target="tpu_custom_call" | custom-call | tf_op jit(solution)/shard_map/update/pallas_call | solution.py:320

commit v3 on v2

--- a/solution.py
+++ b/solution.py
@@ -10,8 +10,8 @@
 MESH = pl.DeviceIdType.MESH
 NZ, NY, NX = 8, 4, 4
 PAIRS = ((0, 0), (0, 1), (1, 1), (0, 2), (1, 2), (2, 2))
-PANELS = 2 * len(PAIRS)
 BLOCK = 64
+GROUPS = ((0, 3), (3, 6))
 
 
 def split(value):
@@ -20,43 +20,45 @@
     return high, low
 
 
-def gram_kernel(modes_ref, batch_ref, gram_ref):
-    @pl.when(pl.program_id(0) == 0)
-    def _():
-        gram_ref[...] = jnp.zeros_like(gram_ref)
-
-    groups = (modes_ref[:, :256], modes_ref[:, 256:], batch_ref[...])
-    parts = [split(group) for group in groups]
-    flipped = [(high.T, low.T) for high, low in parts]
-    for index, (i, j) in enumerate(PAIRS):
-        high_t, low_t = flipped[i]
-        high, low = parts[j]
-        block = jnp.dot(high_t, low, preferred_element_type=jnp.float32)
-        block += jnp.dot(low_t, high, preferred_element_type=jnp.float32)
-        block += jnp.dot(high_t, high, preferred_element_type=jnp.float32)
-        gram_ref[2 * index] += block[:, :128]
-        gram_ref[2 * index + 1] += block[:, 128:]
-
-
-def local_gram(modes, batch, tile=512):
-    rows, width = modes.shape
-    return pl.pallas_call(
-        gram_kernel,
-        grid=(rows // tile,),
-        in_specs=[
-            pl.BlockSpec((tile, width), lambda i: (i, 0)),
-            pl.BlockSpec((tile, batch.shape[1]), lambda i: (i, 0)),
-        ],
-        out_specs=pl.BlockSpec((PANELS, 256, 128), lambda i: (0, 0, 0)),
-        out_shape=jax.ShapeDtypeStruct((PANELS, 256, 128), jnp.float32),
-        compiler_params=pltpu.CompilerParams(dimension_semantics=("arbitrary",)),
-        name="gram",
-    )(modes, batch)
+CHUNKS = 4
+
+
+def load_split(modes, batch, raw_modes, raw_batch, load_sem, parts, flipped):
+    rows = raw_modes.shape[0] // CHUNKS
+    loads = []
+    for i in range(CHUNKS):
+        here = pl.ds(i * rows, rows)
+        loads.append((
+            pltpu.make_async_copy(modes.at[here], raw_modes.at[here], load_sem.at[0, i]),
+            pltpu.make_async_copy(batch.at[here], raw_batch.at[here], load_sem.at[1, i])))
+        for load in loads[-1]:
+            load.start()
+    for i in range(CHUNKS):
+        here = pl.ds(i * rows, rows)
+        for load in loads[i]:
+            load.wait()
+        for g in range(3):
+            group = raw_modes[here, 256 * g:256 * (g + 1)] if g < 2 else raw_batch[here, :]
+            high, low = split(group)
+            parts[0, g, here] = high
+            parts[1, g, here] = low
+            flipped[g, :256, here] = high.T
+            flipped[g, 256:, here] = low.T
+
+
+def gram_block(i, j, parts, flipped):
+    both = jnp.dot(flipped[i], parts[0, j], preferred_element_type=jnp.float32)
+    mixed = both[256:]
+    if i == j:
+        return both[:256] + (mixed + mixed.T)
+    other = jnp.dot(flipped[i, :256], parts[1, j], preferred_element_type=jnp.float32)
+    return both[:256] + (mixed + other)
 
 
 def sum_kernel(
-    part, out, from_core, half, from_first, quarter, from_second, mine, from_z,
-    core_send, core_recv, first_send, first_recv, second_send, second_recv, z_send, z_recv,
+    modes, batch, out, raw_modes, raw_batch, parts, flipped,
+    part, from_core, half, from_first, quarter, from_second, mine, from_near, three, pair, from_far, load_sem,
+    core_send, core_recv, first_send, first_recv, second_send, second_recv, near_send, near_recv, far_send, far_recv,
     gather_second, gather_first, gather_core, arrived,
 ):
     gx, gy = lax.axis_index("gx"), lax.axis_index("gy")
@@ -81,10 +83,9 @@
     peers = [partner]
     peers += [along(0, (x + d) % NX) for d in range(1, NX)]
     peers += [along(1, (y + d) % NY) for d in range(1, NY)]
-    peers += [at_z((z + d) % NZ) for d in range(1, NZ)]
+    peers += [at_z((z + d) % NZ) for d in (1, 2, 3, 5, 6, 7)]
     for peer in peers:
         pl.semaphore_signal(barrier, inc=1, device_id=peer, device_id_type=MESH)
-    pl.semaphore_wait(barrier, len(peers))
 
     sent = []
 
@@ -93,32 +94,53 @@
         sent.append(c)
         return c
 
-    core_copies = {}
-    for d in (2, 1, 3, 0):
+    first_copies = {}
+
+    def keep_half(t, core_copy):
+        core_copy.wait_recv()
+        kept = part[t, core] + from_core[t]
         for p in (0, 1):
-            a = (first[p] + d) % 4
-            core_copies[p, d] = start(copy(
-                part.at[1 - core, p, a], from_core.at[p, a], core_send.at[p, d], core_recv.at[p, d], partner))
-
-    first_copies = {}
-    for d in (2, 1, 3, 0):
-        for p in (0, 1):
-            a = (first[p] + d) % 4
-            core_copies[p, d].wait_recv()
-            half[p, d] = part[core, p, a] + from_core[p, a]
-            if d:
-                first_copies[p, d] = start(copy(
-                    half.at[p, d], from_first.at[p, d - 1], first_send.at[p, d - 1], first_recv.at[p, d - 1],
-                    along(p, a)))
+            for a in range(4):
+                half[p, a, t] = kept[p, a]
+
+    def along_first(group):
+        begin, end = GROUPS[group]
+        for d in (2, 1, 3):
+            for p in (0, 1):
+                a = (first[p] + d) % 4
+                first_copies[group, p, d] = start(copy(
+                    half.at[p, a, pl.ds(begin, end - begin)], from_first.at[p, d - 1, pl.ds(begin, end - begin)],
+                    first_send.at[group, p, d - 1], first_recv.at[group, p, d - 1], along(p, a)))
+
+    load_split(modes, batch, raw_modes, raw_batch, load_sem, parts, flipped)
+    pending = None
+    for t, (i, j) in enumerate(PAIRS):
+        block = gram_block(i, j, parts, flipped)
+        for h in range(2):
+            part[t, h] = block[:, 128 * h:128 * (h + 1)].reshape(2, 4, 4, 8, 128)
+        if t == 0:
+            pl.semaphore_wait(barrier, len(peers))
+        core_copy = start(copy(
+            part.at[t, 1 - core], from_core.at[t], core_send.at[t], core_recv.at[t], partner))
+        if pending is not None:
+            keep_half(t - 1, pending)
+            for group, (begin, end) in enumerate(GROUPS):
+                if end == t:
+                    along_first(group)
+        pending = core_copy
+    keep_half(len(PAIRS) - 1, pending)
+    along_first(len(GROUPS) - 1)
 
     second_copies = {}
     for p in (0, 1):
-        for d in (2, 1, 3):
-            first_copies[p, d].wait_recv()
+        for group in range(len(GROUPS)):
+            for d in (2, 1, 3):
+                first_copies[group, p, d].wait_recv()
         for d in (2, 1, 3, 0):
             b = (second[p] + d) % 4
-            quarter[p, d] = (
-                half[p, 0, b] + from_first[p, 0, b]) + (from_first[p, 1, b] + from_first[p, 2, b])
+            for t in range(len(PAIRS)):
+                quarter[p, d, 8 * t:8 * (t + 1)] = (half[p, first[p], t, b] + from_first[p, 0, t, b]) + (
+                    from_first[p, 1, t, b] + from_first[p, 2, t, b])
             if d:
                 second_copies[p, d] = start(copy(
                     quarter.at[p, d], from_second.at[p, d - 1], second_send.at[p, d - 1],
@@ -130,22 +152,26 @@
         mine[p] = (quarter[p, 0] + from_second[p, 0]) + (from_second[p, 1] + from_second[p, 2])
 
     z_copies = {}
-    for d in (4, 3, 5, 2, 6, 1, 7):
-        z_copies[d] = start(copy(
-            mine, from_z.at[z], z_send.at[d - 1], z_recv.at[d - 1], at_z((z + d) % NZ)))
-    from_z[z] = mine[...]
-    for d in (1, 7, 2, 6, 3, 5, 4):
-        z_copies[d].wait_recv()
-
-    def place(owner, p, a, b):
-        return (owner, p, a, b)
+    for side in (0, 1):
+        z_copies[side] = start(copy(
+            mine, from_near.at[side], near_send.at[side], near_recv.at[side], at_z((z + (1, 7)[side]) % NZ)))
+    for side in (0, 1):
+        z_copies[side].wait_recv()
+    far_copies = []
+    for p in (0, 1):
+        two = mine[p] + from_near[1 - p, p]
+        pair[p] = two
+        three[p] = two + from_near[p, p]
+        far_copies.append(start(copy(
+            three.at[p], from_far.at[p, 0], far_send.at[p, 0], far_recv.at[p, 0], at_z((z + (3, 5)[p]) % NZ))))
+        far_copies.append(start(copy(
+            pair.at[p], from_far.at[p, 1], far_send.at[p, 1], far_recv.at[p, 1], at_z((z + (6, 2)[p]) % NZ))))
+    for c in far_copies:
+        c.wait_recv()
 
     for p in (0, 1):
         here = (core, p, first[p], second[p])
-        total = from_z[0, p]
-        for index in range(1, NZ):
-            total = total + from_z[index, p]
-        out[here] = total
+        out[here] = three[p] + (from_far[p, 0] + from_far[p, 1])
         for d in (2, 1, 3):
             start(copy(out.at[here], out.at[here], gather_second.at[p, d - 1], arrived.at[here],
                        along(1 - p, (second[p] + d) % 4)))
@@ -181,36 +207,50 @@
         c.wait_send()
 
 
-def global_sum(part):
-    rows = part.shape[0] * part.shape[1] // 64
-    f32 = jnp.float32
-    vmem = pl.BlockSpec(memory_space=pltpu.VMEM)
+def gram_sum(modes, batch):
+    rows = 8 * len(PAIRS)
+    blocks = len(PAIRS)
+    f32, b16 = jnp.float32, jnp.bfloat16
     dma = pltpu.SemaphoreType.DMA
-    out = pl.pallas_call(
+    return pl.pallas_call(
         sum_kernel,
-        in_specs=[vmem],
-        out_specs=vmem,
+        in_specs=[pl.BlockSpec(memory_space=pl.ANY)] * 2,
+        out_specs=pl.BlockSpec(memory_space=pltpu.VMEM),
         out_shape=jax.ShapeDtypeStruct((2, 2, 4, 4, rows, 128), f32),
         scratch_shapes=[
-            pltpu.VMEM((2, 4, 4, rows, 128), f32),
-            pltpu.VMEM((2, 4, 4, rows, 128), f32),
-            pltpu.VMEM((2, 3, 4, rows, 128), f32),
+            pltpu.VMEM(modes.shape, f32),
+            pltpu.VMEM(batch.shape, f32),
+            pltpu.VMEM((2, 3, modes.shape[0], 256), b16),
+            pltpu.VMEM((3, 512, modes.shape[0]), b16),
+            pltpu.VMEM((blocks, 2, 2, 4, 4, 8, 128), f32),
+            pltpu.VMEM((blocks, 2, 4, 4, 8, 128), f32),
+            pltpu.VMEM((2, 4, blocks, 4, 8, 128), f32),
+            pltpu.VMEM((2, 3, blocks, 4, 8, 128), f32),
             pltpu.VMEM((2, 4, rows, 128), f32),
             pltpu.VMEM((2, 3, rows, 128), f32),
             pltpu.VMEM((2, rows, 128), f32),
-            pltpu.VMEM((NZ, 2, rows, 128), f32),
-            dma((2, 4)), dma((2, 4)), dma((2, 3)), dma((2, 3)), dma((2, 3)), dma((2, 3)),
-            dma((NZ - 1,)), dma((NZ - 1,)),
+            pltpu.VMEM((2, 2, rows, 128), f32),
+            pltpu.VMEM((2, rows, 128), f32),
+            pltpu.VMEM((2, rows, 128), f32),
+            pltpu.VMEM((2, 2, rows, 128), f32),
+            dma((2, CHUNKS)),
+            dma((blocks,)), dma((blocks,)), dma((len(GROUPS), 2, 3)), dma((len(GROUPS), 2, 3)), dma((2, 3)), dma((2, 3)),
+            dma((2,)), dma((2,)), dma((2, 2)), dma((2, 2)),
             dma((2, 3)), dma((2, 4, 3)), dma((2, 4, 4)), dma((2, 2, 4, 4)),
         ],
         compiler_params=pltpu.CompilerParams(collective_id=0, has_side_effects=True),
-        name="global_sum",
-    )(part.reshape(2, 2, 4, 4, rows, 128))
-    return out.reshape(part.shape)
+        name="gram_sum",
+    )(modes, batch)
 
 
 def exact_dot(a, b, dims=((1,), (0,))):
-    return lax.dot_general(a, b, (dims, ((), ())), precision=lax.Precision.HIGHEST, preferred_element_type=jnp.float32)
+    (a_high, a_low), (b_high, b_low) = split(a), split(b)
+
+    def dot(left, right):
+        return lax.dot_general(left, right, (dims, ((), ())), preferred_element_type=jnp.float32)
+
+    return dot(a_high, b_high) + (dot(a_low, b_high) + dot(a_high, b_low))
+
 
 def lanes(value, index):
     return jnp.broadcast_to(value[:, index:index + 1], value.shape)
@@ -283,7 +323,8 @@
     @pl.when(pl.program_id(0) == 0)
     def _():
         def block(index):
-            return jnp.concatenate([sums_ref[2 * index], sums_ref[2 * index + 1]], axis=1)
+            panels = [sums_ref[h, :, :, :, 8 * index:8 * (index + 1), :].reshape(n, n // 2) for h in range(2)]
+            return jnp.concatenate(panels, axis=1)
 
         first, second = block(3), block(4)
         coeffs = (first * (1.0 / total_rows), second * (1.0 / total_rows))
@@ -303,25 +344,25 @@
             top = core_ref[n * i:n * (i + 1), :] - exact_dot(coeffs[i], weights)
             high[n * i:n * (i + 1), :], low[n * i:n * (i + 1), :] = split(top)
 
-    modes_high, modes_low = split(modes_ref[...])
-    batch_high, batch_low = split(batch_ref[...])
-
-    def times(left, right):
-        return jnp.dot(left, right, preferred_element_type=jnp.float32)
-
-    small = times(modes_low, high[:width, :]) + times(batch_low, high[width:, :])
-    small += times(modes_high, low[:width, :]) + times(batch_high, low[width:, :])
-    out_ref[...] = small + times(modes_high, high[:width, :]) + times(batch_high, high[width:, :])
-
-
-def update(sums, core, modes, batch, total_rows, tile=256):
+    values = [split(value) for value in (modes_ref[:, :n], modes_ref[:, n:], batch_ref[...])]
+    stacked = jnp.concatenate(
+        [jnp.concatenate([v[half] for v in values], axis=1) for half in (0, 1)], axis=0)
+    rows = out_ref.shape[0]
+    for i in range(width // n):
+        columns = slice(n * i, n * (i + 1))
+        both = jnp.dot(stacked, high[:, columns], preferred_element_type=jnp.float32)
+        other = jnp.dot(stacked[:rows], low[:, columns], preferred_element_type=jnp.float32)
+        out_ref[:, columns] = both[:rows] + (both[rows:] + other)
+
+
+def update(sums, core, modes, batch, total_rows, tile=512):
     rows, width = modes.shape
     n = batch.shape[1]
     return pl.pallas_call(
         functools.partial(update_kernel, total_rows),
         grid=(rows // tile,),
         in_specs=[
-            pl.BlockSpec(sums.shape, lambda i: (0, 0, 0), pipeline_mode=pl.Buffered(1)),
+            pl.BlockSpec(sums.shape, lambda i: (0,) * 6, pipeline_mode=pl.Buffered(1)),
             pl.BlockSpec(core.shape, lambda i: (0, 0), pipeline_mode=pl.Buffered(1)),
             pl.BlockSpec((tile, width), lambda i: (i, 0)),
             pl.BlockSpec((tile, n), lambda i: (i, 0)),
@@ -340,7 +381,7 @@
 
 def shards(modes, batch, core):
     total_rows = modes.shape[0] * lax.axis_size("gx") * lax.axis_size("gy")
-    return update(global_sum(local_gram(modes, batch)), core, modes, batch, total_rows)
+    return update(gram_sum(modes, batch), core, modes, batch, total_rows)
 
 
 def solution(mesh):

time: 79.3 us -> 71.4 us (0.900)
  Pallas kernels: 79 us -> 71.2 us
    pallas_call x1, Pallas kernels: 24.3 us -> 20.2 us  [update(): pl.pallas_call(functools.partial(update_kernel, total_rows), grid=(rows /...]
    pallas_call x2 -> x1, Pallas kernels: 54.7 us -> 51 us  [gram_sum(): pl.pallas_call(sum_kernel, in_specs=[pl.BlockSpec(memory_space=pl.ANY)] *...]
where the time goes in v3:
time: 71.4 us; the launch traced here: 71.2 us
  Pallas kernels  71.2 us (100%)
    pallas_call x1, Pallas kernels, gram_sum(): pl.pallas_call(sum_kernel, in_specs=[pl.BlockSpec(memory_space=pl.ANY)] *...  51 us
    pallas_call x1, Pallas kernels, update(): pl.pallas_call(functools.partial(update_kernel, total_rows), grid=(rows /...  20.2 us

profile of v3, /device:TPU:1, one launch (start us, length us, event | category | flops | bytes accessed | tf_op | source)
XLA Modules:
  0.0 71.2 jit_solution(13393738641401978179)
XLA Ops:
  0.0 51.0 %gram_sum.1.sums_ref = f32[2,2,4,4,48,128]{5,4,3,2,1,0:T(8,128)} custom-call(f32[2048,512]{1,0:T(8,128)} %modes_ref.1, f32[2048,256]{1,0:T(8,128)} %batch_ref.1), custom_call_target="tpu_custom_call" | custom-call | tf_op jit(solution)/shard_map/gram_sum/pallas_call | solution.py:215
  51.0 20.2 %update.1 = f32[2048,512]{1,0:T(8,128)} custom-call(f32[2,2,4,4,48,128]{5,4,3,2,1,0:T(8,128)} %gram_sum.1.sums_ref, f32[768,512]{1,0:T(8,128)} %core_ref.1, f32[2048,512]{1,0:T(8,128)} %modes_ref.1, f32[2048,256]{1,0:T(8,128)} %batch_ref.1), custom_call_target="tpu_custom_call" | custom-call | tf_op jit(solution)/shard_map/update/pallas_call | solution.py:361

commit v4 on v3

--- a/solution.py
+++ b/solution.py
@@ -20,30 +20,16 @@
     return high, low
 
 
-CHUNKS = 4
-
-
-def load_split(modes, batch, raw_modes, raw_batch, load_sem, parts, flipped):
-    rows = raw_modes.shape[0] // CHUNKS
-    loads = []
-    for i in range(CHUNKS):
-        here = pl.ds(i * rows, rows)
-        loads.append((
-            pltpu.make_async_copy(modes.at[here], raw_modes.at[here], load_sem.at[0, i]),
-            pltpu.make_async_copy(batch.at[here], raw_batch.at[here], load_sem.at[1, i])))
-        for load in loads[-1]:
-            load.start()
-    for i in range(CHUNKS):
-        here = pl.ds(i * rows, rows)
-        for load in loads[i]:
-            load.wait()
-        for g in range(3):
-            group = raw_modes[here, 256 * g:256 * (g + 1)] if g < 2 else raw_batch[here, :]
-            high, low = split(group)
-            parts[0, g, here] = high
-            parts[1, g, here] = low
-            flipped[g, :256, here] = high.T
-            flipped[g, 256:, here] = low.T
+def split_group(g, modes, batch, parts, flipped):
+    rows = modes.shape[0]
+    step = rows // 4
+    for i in range(4):
+        here = pl.ds(i * step, step)
+        high, low = split(modes[here, 256 * g:256 * (g + 1)] if g < 2 else batch[here, :])
+        parts[0, g, here] = high
+        parts[1, g, here] = low
+        flipped[g, :256, here] = high.T
+        flipped[g, 256:, here] = low.T
 
 
 def gram_block(i, j, parts, flipped):
@@ -56,8 +42,8 @@
 
 
 def sum_kernel(
-    modes, batch, out, raw_modes, raw_batch, parts, flipped,
-    part, from_core, half, from_first, quarter, from_second, mine, from_near, three, pair, from_far, load_sem,
+    modes, batch, out, parts, flipped,
+    part, from_core, half, from_first, quarter, from_second, mine, from_near, three, pair, from_far,
     core_send, core_recv, first_send, first_recv, second_send, second_recv, near_send, near_recv, far_send, far_recv,
     gather_second, gather_first, gather_core, arrived,
 ):
@@ -112,9 +98,11 @@
                     half.at[p, a, pl.ds(begin, end - begin)], from_first.at[p, d - 1, pl.ds(begin, end - begin)],
                     first_send.at[group, p, d - 1], first_recv.at[group, p, d - 1], along(p, a)))
 
-    load_split(modes, batch, raw_modes, raw_batch, load_sem, parts, flipped)
+    split_group(0, modes, batch, parts, flipped)
     pending = None
     for t, (i, j) in enumerate(PAIRS):
+        if t < 2:
+            split_group(t + 1, modes, batch, parts, flipped)
         block = gram_block(i, j, parts, flipped)
         for h in range(2):
             part[t, h] = block[:, 128 * h:128 * (h + 1)].reshape(2, 4, 4, 8, 128)
@@ -214,12 +202,10 @@
     dma = pltpu.SemaphoreType.DMA
     return pl.pallas_call(
         sum_kernel,
-        in_specs=[pl.BlockSpec(memory_space=pl.ANY)] * 2,
+        in_specs=[pl.BlockSpec(memory_space=pltpu.VMEM)] * 2,
         out_specs=pl.BlockSpec(memory_space=pltpu.VMEM),
         out_shape=jax.ShapeDtypeStruct((2, 2, 4, 4, rows, 128), f32),
         scratch_shapes=[
-            pltpu.VMEM(modes.shape, f32),
-            pltpu.VMEM(batch.shape, f32),
             pltpu.VMEM((2, 3, modes.shape[0], 256), b16),
             pltpu.VMEM((3, 512, modes.shape[0]), b16),
             pltpu.VMEM((blocks, 2, 2, 4, 4, 8, 128), f32),
@@ -233,12 +219,12 @@
             pltpu.VMEM((2, rows, 128), f32),
             pltpu.VMEM((2, rows, 128), f32),
             pltpu.VMEM((2, 2, rows, 128), f32),
-            dma((2, CHUNKS)),
             dma((blocks,)), dma((blocks,)), dma((len(GROUPS), 2, 3)), dma((len(GROUPS), 2, 3)), dma((2, 3)), dma((2, 3)),
             dma((2,)), dma((2,)), dma((2, 2)), dma((2, 2)),
             dma((2, 3)), dma((2, 4, 3)), dma((2, 4, 4)), dma((2, 2, 4, 4)),
         ],
-        compiler_params=pltpu.CompilerParams(collective_id=0, has_side_effects=True),
+        compiler_params=pltpu.CompilerParams(
+            collective_id=0, has_side_effects=True, vmem_limit_bytes=36 * 2**20),
         name="gram_sum",
     )(modes, batch)
 
@@ -374,7 +360,8 @@
             pltpu.VMEM(core.shape, jnp.bfloat16),
             pltpu.VMEM(core.shape, jnp.bfloat16),
         ],
-        compiler_params=pltpu.CompilerParams(dimension_semantics=("arbitrary",)),
+        compiler_params=pltpu.CompilerParams(
+            dimension_semantics=("arbitrary",), vmem_limit_bytes=24 * 2**20),
         name="update",
     )(sums, core, modes, batch)
 

time: 71.4 us -> 68.7 us (0.962)
  Pallas kernels: 71.2 us -> 64.8 us
  local copies, waits for them, and re-layouts: 0 us -> 3.78 us
    unnamed x0 -> x6, local copies, waits for them, and re-layouts: none -> 3.78 us
    pallas_call x1, Pallas kernels: 51 us -> 47.4 us  [gram_sum(): pl.pallas_call(sum_kernel, in_specs=[pl.BlockSpec(memory_space=pltpu.VMEM...]
    pallas_call x1, Pallas kernels: 20.2 us -> 17.4 us  [update(): pl.pallas_call(functools.partial(update_kernel, total_rows), grid=(rows /...]
where the time goes in v4:
time: 68.7 us; the launch traced here: 68.6 us
  Pallas kernels  64.8 us (94%)
  local copies, waits for them, and re-layouts  3.78 us (6%)
    pallas_call x1, Pallas kernels, gram_sum(): pl.pallas_call(sum_kernel, in_specs=[pl.BlockSpec(memory_space=pltpu.VMEM...  47.4 us
    pallas_call x1, Pallas kernels, update(): pl.pallas_call(functools.partial(update_kernel, total_rows), grid=(rows /...  17.4 us
    unnamed x6, local copies, waits for them, and re-layouts  3.78 us

profile of v4, /device:TPU:1, one launch (start us, length us, event | category | flops | bytes accessed | tf_op | source)
XLA Modules:
  0.0 68.6 jit_solution(3696442625037755991)
XLA Ops:
  0.0 0.0 copy-start
  0.0 2.2 %copy-done = f32[2048,512]{1,0:T(8,128)S(1)} copy-done((f32[2048,512]{1,0:T(8,128)S(1)}, f32[2048,512]{1,0:T(8,128)}, u32[]{:S(2)}) %copy-start) | copy-done | bytes 4194328
  2.2 0.0 copy-start.1
  2.2 1.6 %copy-done.1 = f32[2048,256]{1,0:T(8,128)S(1)} copy-done((f32[2048,256]{1,0:T(8,128)S(1)}, f32[2048,256]{1,0:T(8,128)}, u32[]{:S(2)}) %copy-start.1) | copy-done | bytes 2097176
  3.8 0.0 copy-start.2
  3.8 47.4 %gram_sum.1.sums_ref = f32[2,2,4,4,48,128]{5,4,3,2,1,0:T(8,128)S(1)} custom-call(f32[2048,512]{1,0:T(8,128)S(1)} %copy-done, f32[2048,256]{1,0:T(8,128)S(1)} %copy-done.1), custom_call_target="tpu_custom_call" | custom-call | tf_op jit(solution)/shard_map/gram_sum/pallas_call | solution.py:203
  51.2 0.0 copy-done.2
  51.2 17.4 %update.1 = f32[2048,512]{1,0:T(8,128)} custom-call(f32[2,2,4,4,48,128]{5,4,3,2,1,0:T(8,128)S(1)} %gram_sum.1.sums_ref, f32[768,512]{1,0:T(8,128)S(1)} %copy-done.2, f32[2048,512]{1,0:T(8,128)S(1)} %copy-done, f32[2048,256]{1,0:T(8,128)S(1)} %copy-done.1), custom_call_target="tpu_custom_call" | custom-call | tf_op jit(solution)/shard_map/update/pallas_call | solution.py:347
Async XLA Ops:
  0.0 2.2 %copy-start = (f32[2048,512]{1,0:T(8,128)S(1)}, f32[2048,512]{1,0:T(8,128)}, u32[]{:S(2)}) copy-start(f32[2048,512]{1,0:T(8,128)} %modes_ref.1) | copy-start | bytes 12582916
  2.2 1.6 %copy-start.1 = (f32[2048,256]{1,0:T(8,128)S(1)}, f32[2048,256]{1,0:T(8,128)}, u32[]{:S(2)}) copy-start(f32[2048,256]{1,0:T(8,128)} %batch_ref.1) | copy-start | bytes 6291460
  3.8 47.4 %copy-start.2 = (f32[768,512]{1,0:T(8,128)S(1)}, f32[768,512]{1,0:T(8,128)}, u32[]{:S(2)}) copy-start(f32[768,512]{1,0:T(8,128)} %core_ref.1) | copy-start | bytes 4718596

commit v5 on v4

--- a/solution.py
+++ b/solution.py
@@ -20,12 +20,27 @@
     return high, low
 
 
-def split_group(g, modes, batch, parts, flipped):
-    rows = modes.shape[0]
-    step = rows // 4
-    for i in range(4):
+LOADS = 2
+
+
+def loads(modes, batch, raw, load_sem):
+    step = raw.shape[1] // LOADS
+    copies = []
+    for g in range(3):
+        for i in range(LOADS):
+            here = pl.ds(i * step, step)
+            source = modes.at[here, pl.ds(256 * g, 256)] if g < 2 else batch.at[here]
+            copies.append(pltpu.make_async_copy(source, raw.at[g, here], load_sem.at[g, i]))
+    return copies
+
+
+def split_group(g, copies, raw, parts, flipped):
+    rows = raw.shape[1]
+    step = rows // LOADS
+    for i in range(LOADS):
+        copies[LOADS * g + i].wait()
         here = pl.ds(i * step, step)
-        high, low = split(modes[here, 256 * g:256 * (g + 1)] if g < 2 else batch[here, :])
+        high, low = split(raw[g, here])
         parts[0, g, here] = high
         parts[1, g, here] = low
         flipped[g, :256, here] = high.T
@@ -42,7 +57,7 @@
 
 
 def sum_kernel(
-    modes, batch, out, parts, flipped,
+    modes, batch, out, parts, raw, load_sem, flipped,
     part, from_core, half, from_first, quarter, from_second, mine, from_near, three, pair, from_far,
     core_send, core_recv, first_send, first_recv, second_send, second_recv, near_send, near_recv, far_send, far_recv,
     gather_second, gather_first, gather_core, arrived,
@@ -65,6 +80,9 @@
             device_id=device, device_id_type=MESH,
         )
 
+    copies = loads(modes, batch, raw, load_sem)
+    for c in copies:
+        c.start()
     barrier = pltpu.get_barrier_semaphore()
     peers = [partner]
     peers += [along(0, (x + d) % NX) for d in range(1, NX)]
@@ -98,11 +116,11 @@
                     half.at[p, a, pl.ds(begin, end - begin)], from_first.at[p, d - 1, pl.ds(begin, end - begin)],
                     first_send.at[group, p, d - 1], first_recv.at[group, p, d - 1], along(p, a)))
 
-    split_group(0, modes, batch, parts, flipped)
+    split_group(0, copies, raw, parts, flipped)
     pending = None
     for t, (i, j) in enumerate(PAIRS):
         if t < 2:
-            split_group(t + 1, modes, batch, parts, flipped)
+            split_group(t + 1, copies, raw, parts, flipped)
         block = gram_block(i, j, parts, flipped)
         for h in range(2):
             part[t, h] = block[:, 128 * h:128 * (h + 1)].reshape(2, 4, 4, 8, 128)
@@ -202,11 +220,15 @@
     dma = pltpu.SemaphoreType.DMA
     return pl.pallas_call(
         sum_kernel,
-        in_specs=[pl.BlockSpec(memory_space=pltpu.VMEM)] * 2,
-        out_specs=pl.BlockSpec(memory_space=pltpu.VMEM),
-        out_shape=jax.ShapeDtypeStruct((2, 2, 4, 4, rows, 128), f32),
+        in_specs=[pl.BlockSpec(memory_space=pltpu.HBM)] * 2,
+        out_specs=[pl.BlockSpec(memory_space=pltpu.VMEM)] * 2,
+        out_shape=[
+            jax.ShapeDtypeStruct((2, 2, 4, 4, rows, 128), f32),
+            jax.ShapeDtypeStruct((2, 3, modes.shape[0], 256), b16),
+        ],
         scratch_shapes=[
-            pltpu.VMEM((2, 3, modes.shape[0], 256), b16),
+            pltpu.VMEM((3, modes.shape[0], 256), f32),
+            dma((3, LOADS)),
             pltpu.VMEM((3, 512, modes.shape[0]), b16),
             pltpu.VMEM((blocks, 2, 2, 4, 4, 8, 128), f32),
             pltpu.VMEM((blocks, 2, 4, 4, 8, 128), f32),
@@ -302,9 +324,9 @@
             upd = exact_dot(rest, new, ((0,), (0,)))
             aug[o + BLOCK:, :] = aug[o + BLOCK:, :] - upd[o + BLOCK:, :]
 
-def update_kernel(total_rows, sums_ref, core_ref, modes_ref, batch_ref, out_ref, aug, high, low):
-    width = modes_ref.shape[1]
-    n = batch_ref.shape[1]
+def update_kernel(total_rows, sums_ref, core_ref, parts_ref, out_ref, aug, high, low):
+    width = core_ref.shape[1]
+    n = core_ref.shape[0] - width
 
     @pl.when(pl.program_id(0) == 0)
     def _():
@@ -330,9 +352,8 @@
             top = core_ref[n * i:n * (i + 1), :] - exact_dot(coeffs[i], weights)
             high[n * i:n * (i + 1), :], low[n * i:n * (i + 1), :] = split(top)
 
-    values = [split(value) for value in (modes_ref[:, :n], modes_ref[:, n:], batch_ref[...])]
     stacked = jnp.concatenate(
-        [jnp.concatenate([v[half] for v in values], axis=1) for half in (0, 1)], axis=0)
+        [jnp.concatenate([parts_ref[half, g] for g in range(3)], axis=1) for half in (0, 1)], axis=0)
     rows = out_ref.shape[0]
     for i in range(width // n):
         columns = slice(n * i, n * (i + 1))
@@ -341,17 +362,16 @@
         out_ref[:, columns] = both[:rows] + (both[rows:] + other)
 
 
-def update(sums, core, modes, batch, total_rows, tile=512):
-    rows, width = modes.shape
-    n = batch.shape[1]
+def update(sums, core, parts, total_rows, tile=512):
+    rows, width = parts.shape[2], core.shape[1]
+    n = core.shape[0] - width
     return pl.pallas_call(
         functools.partial(update_kernel, total_rows),
         grid=(rows // tile,),
         in_specs=[
             pl.BlockSpec(sums.shape, lambda i: (0,) * 6, pipeline_mode=pl.Buffered(1)),
             pl.BlockSpec(core.shape, lambda i: (0, 0), pipeline_mode=pl.Buffered(1)),
-            pl.BlockSpec((tile, width), lambda i: (i, 0)),
-            pl.BlockSpec((tile, n), lambda i: (i, 0)),
+            pl.BlockSpec((2, 3, tile, 256), lambda i: (0, 0, i, 0)),
         ],
         out_specs=pl.BlockSpec((tile, width), lambda i: (i, 0)),
         out_shape=jax.ShapeDtypeStruct((rows, width), jnp.float32),
@@ -363,12 +383,15 @@
         compiler_params=pltpu.CompilerParams(
             dimension_semantics=("arbitrary",), vmem_limit_bytes=24 * 2**20),
         name="update",
-    )(sums, core, modes, batch)
+    )(sums, core, parts)
 
 
 def shards(modes, batch, core):
     total_rows = modes.shape[0] * lax.axis_size("gx") * lax.axis_size("gy")
-    return update(gram_sum(modes, batch), core, modes, batch, total_rows)
+    modes = pltpu.with_memory_space_constraint(modes, pltpu.HBM)
+    batch = pltpu.with_memory_space_constraint(batch, pltpu.HBM)
+    sums, parts = gram_sum(modes, batch)
+    return update(sums, core, parts, total_rows)
 
 
 def solution(mesh):

time: 68.7 us -> 67.1 us (0.977)
  local copies, waits for them, and re-layouts: 3.78 us -> 0.01 us
  Pallas kernels: 64.8 us -> 67 us
    unnamed x6 -> x2, local copies, waits for them, and re-layouts: 3.78 us -> 0.01 us
    pallas_call x1, Pallas kernels: 47.4 us -> 49.2 us  [gram_sum(): pl.pallas_call(sum_kernel, in_specs=[pl.BlockSpec(memory_space=pltpu.HBM)...]
where the time goes in v5:
time: 67.1 us; the launch traced here: 67 us
  Pallas kernels  67 us (100%)
    pallas_call x1, Pallas kernels, gram_sum(): pl.pallas_call(sum_kernel, in_specs=[pl.BlockSpec(memory_space=pltpu.HBM)...  49.2 us
    pallas_call x1, Pallas kernels, update(): pl.pallas_call(functools.partial(update_kernel, total_rows), grid=(rows /...  17.8 us

profile of v5, /device:TPU:1, one launch (start us, length us, event | category | flops | bytes accessed | tf_op | source)
XLA Modules:
  0.0 67.0 jit_solution(12905058269061299468)
XLA Ops:
  0.0 0.0 copy-start
  0.0 49.2 %gram_sum.1 = (f32[2,2,4,4,48,128]{5,4,3,2,1,0:T(8,128)S(1)}, bf16[2,3,2048,256]{3,2,1,0:T(8,128)(2,1)S(1)}) custom-call(f32[2048,512]{1,0:T(8,128)} %modes.1, f32[2048,256]{1,0:T(8,128)} %batch.1), custom_call_target="tpu_custom_call" | custom-call | tf_op jit(solution)/shard_map/gram_sum/pallas_call | solution.py:221
  49.2 0.0 copy-done
  49.2 17.8 %update.1 = f32[2048,512]{1,0:T(8,128)} custom-call(f32[2,2,4,4,48,128]{5,4,3,2,1,0:T(8,128)S(1)} %get-tuple-element.7.sums_ref, f32[768,512]{1,0:T(8,128)S(1)} %copy-done, bf16[2,3,2048,256]{3,2,1,0:T(8,128)(2,1)S(1)} %get-tuple-element.8.parts_ref), custom_call_target="tpu_custom_call" | custom-call | tf_op jit(solution)/shard_map/update/pallas_call | solution.py:368
Async XLA Ops:
  0.0 49.2 %copy-start = (f32[768,512]{1,0:T(8,128)S(1)}, f32[768,512]{1,0:T(8,128)}, u32[]{:S(2)}) copy-start(f32[768,512]{1,0:T(8,128)} %core_ref.1) | copy-start | bytes 4718596

commit v6 on v5

--- a/solution.py
+++ b/solution.py
@@ -11,7 +11,7 @@
 NZ, NY, NX = 8, 4, 4
 PAIRS = ((0, 0), (0, 1), (1, 1), (0, 2), (1, 2), (2, 2))
 BLOCK = 64
-GROUPS = ((0, 3), (3, 6))
+GROUPS = ((0, 4), (4, 6))
 
 
 def split(value):
@@ -317,12 +317,14 @@
         if not odd:
             w = pltpu.roll(w, 64, 1)
         z = w[:, :64]
-        new = exact_dot(z, aug[o:o + BLOCK, :])
-        aug[o:o + BLOCK, :] = new
+        begin = (o + BLOCK) // 128 * 128
+        end = n + (o + BLOCK + 127) // 128 * 128
+        new = exact_dot(z, aug[o:o + BLOCK, begin:end])
+        aug[o:o + BLOCK, begin:end] = new
         if o + BLOCK < n:
-            rest = new[:, :n]
-            upd = exact_dot(rest, new, ((0,), (0,)))
-            aug[o + BLOCK:, :] = aug[o + BLOCK:, :] - upd[o + BLOCK:, :]
+            change = exact_dot(new[:, :n - begin], new, ((0,), (0,)))
+            aug[o + BLOCK:, begin:end] = aug[o + BLOCK:, begin:end] - change[o + BLOCK - begin:, :]
+
 
 def update_kernel(total_rows, sums_ref, core_ref, parts_ref, out_ref, aug, high, low):
     width = core_ref.shape[1]

time: 67.1 us -> 66.4 us (0.990)
  Pallas kernels: 67 us -> 66.3 us
where the time goes in v6:
time: 66.4 us
  Pallas kernels  66.3 us (100%)
    pallas_call x1, Pallas kernels, gram_sum(): pl.pallas_call(sum_kernel, in_specs=[pl.BlockSpec(memory_space=pltpu.HBM)...  48.7 us
    pallas_call x1, Pallas kernels, update(): pl.pallas_call(functools.partial(update_kernel, total_rows), grid=(rows /...  17.7 us

profile of v6, /device:TPU:1, one launch (start us, length us, event | category | flops | bytes accessed | tf_op | source)
XLA Modules:
  0.0 66.4 jit_solution(13653774739235293259)
XLA Ops:
  0.0 0.0 copy-start
  0.0 48.7 %gram_sum.1 = (f32[2,2,4,4,48,128]{5,4,3,2,1,0:T(8,128)S(1)}, bf16[2,3,2048,256]{3,2,1,0:T(8,128)(2,1)S(1)}) custom-call(f32[2048,512]{1,0:T(8,128)} %modes.1, f32[2048,256]{1,0:T(8,128)} %batch.1), custom_call_target="tpu_custom_call" | custom-call | tf_op jit(solution)/shard_map/gram_sum/pallas_call | solution.py:221
  48.7 0.0 copy-done
  48.7 17.7 %update.1 = f32[2048,512]{1,0:T(8,128)} custom-call(f32[2,2,4,4,48,128]{5,4,3,2,1,0:T(8,128)S(1)} %get-tuple-element.7.sums_ref, f32[768,512]{1,0:T(8,128)S(1)} %copy-done, bf16[2,3,2048,256]{3,2,1,0:T(8,128)(2,1)S(1)} %get-tuple-element.8.parts_ref), custom_call_target="tpu_custom_call" | custom-call | tf_op jit(solution)/shard_map/update/pallas_call | solution.py:370
Async XLA Ops:
  0.0 48.7 %copy-start = (f32[768,512]{1,0:T(8,128)S(1)}, f32[768,512]{1,0:T(8,128)}, u32[]{:S(2)}) copy-start(f32[768,512]{1,0:T(8,128)} %core_ref.1) | copy-start | bytes 4718596
